TPU v7x, 32 devices: a whole 2x2x4 slice. The times are simulated.
32 devices in a mesh: rep: 8 (over z, x), shard: 4 (over y, core).
Axes of the slice: x: 2, y: 2, z: 4, core: 2. Of those that a mesh axis runs over, the one named last changes fastest.
Arguments:
- latent_tokens: bfloat16 [256, 256, 384], P(('rep', 'shard')), may hold values from -6 to 6
- cond: bfloat16 [256, 384], P(('rep', 'shard')), may hold values from -6 to 6
- w_ada: bfloat16 [384, 2304], P('shard'), may hold values from -0.3125 to 0.3125
- b_ada: bfloat16 [2304], P('shard'), may hold values from -3 to 3
- w_qkv: bfloat16 [384, 1152], P('shard'), may hold values from -0.3125 to 0.3125
- b_qv: bfloat16 [768], P('shard'), may hold values from -3 to 3
- w_o: bfloat16 [384, 384], P('shard'), may hold values from -0.875 to 0.875
- b_o: bfloat16 [384], P('shard'), may hold values from -3 to 3
- w_1: bfloat16 [384, 1536], P('shard'), may hold values from -0.3125 to 0.3125
- b_1: bfloat16 [1536], P('shard'), may hold values from -3 to 3
- w_2: bfloat16 [1536, 384], P('shard'), may hold values from -0.15625 to 0.15625
- b_2: bfloat16 [384], P('shard'), may hold values from -3 to 3
- grad_out: bfloat16 [256, 256, 384], P(('rep', 'shard')), may hold values from -6 to 6
Outputs:
- block_out: bfloat16 [256, 256, 384], P(('rep', 'shard'))
- grad_tokens: float32 [256, 256, 384], P(('rep', 'shard'))
- grad_cond: float32 [256, 384], P(('rep', 'shard'))
- grad_w_ada: float32 [384, 2304], P('shard')
- grad_b_ada: float32 [2304], P('shard')
- grad_w_qkv: float32 [384, 1152], P('shard')
- grad_b_qv: float32 [768], P('shard')
- grad_w_o: float32 [384, 384], P('shard')
- grad_b_o: float32 [384], P('shard')
- grad_w_1: float32 [384, 1536], P('shard')
- grad_b_1: float32 [1536], P('shard')
- grad_w_2: float32 [1536, 384], P('shard')
- grad_b_2: float32 [384], P('shard')
All inputs are finite; a program needn't handle non-finite values.
Results may differ from a plain program's by a relative error of at most 0.019.
The roundings to bfloat16 on the way count: a program that leaves them out, or rounds other values in their place, can miss the bound.
Values may be sent and summed in bfloat16 or wider, within the bound.
No kernel may reach another device: no remote copies, remote signals or barrier semaphores. Data moves between devices by JAX's collectives and lax.ppermute only.
A program may use at most 128 MiB of HBM per device.

v0:
```python
import math
import jax
import jax.numpy as jnp
from jax import lax
from jax.sharding import PartitionSpec as P

HEADS = 6


def layer_norm(value):
    centred = value - jnp.mean(value, axis=-1, keepdims=True)
    factor = lax.rsqrt(jnp.mean(centred * centred, axis=-1, keepdims=True) + 1e-06)
    return (centred * factor, factor)


def norm_back(normed, factor, grad_normed):
    inner = jnp.mean(grad_normed, axis=-1, keepdims=True)
    along = jnp.mean(grad_normed * normed, axis=-1, keepdims=True)
    return factor * (grad_normed - inner - normed * along)


def project(left, right):
    return jnp.einsum("lsd,de->lse", left, right, preferred_element_type=jnp.float32)


def weight_grad(left, right):
    return jnp.einsum("lsd,lse->de", left, right, preferred_element_type=jnp.float32)


def attend(items):
    query, key, value = items
    scores = jnp.einsum("lqhd,lkhd->lhqk", query, key, preferred_element_type=jnp.float32) * 0.125
    top = jnp.max(scores, axis=-1, keepdims=True)
    expo = jnp.exp(scores - top)
    total = jnp.sum(expo, axis=-1, keepdims=True)
    probs = (expo / total).astype(jnp.bfloat16)
    attended = jnp.einsum("lhqk,lkhd->lqhd", probs, value, preferred_element_type=jnp.float32)
    return (attended.astype(jnp.bfloat16), top + jnp.log(total))


def attend_back(items):
    query, key, value, logsum, grad_att = items
    scores = jnp.einsum("lqhd,lkhd->lhqk", query, key, preferred_element_type=jnp.float32) * 0.125
    probs = jnp.exp(scores - logsum)
    rounded = probs.astype(jnp.bfloat16)
    grad_value = jnp.einsum(
        "lhqk,lqhd->lkhd", rounded, grad_att, preferred_element_type=jnp.float32
    )
    grad_probs = jnp.einsum("lqhd,lkhd->lhqk", grad_att, value, preferred_element_type=jnp.float32)
    row_total = jnp.sum(probs * grad_probs, axis=-1, keepdims=True)
    grad_scores = (probs * (grad_probs - row_total)).astype(jnp.bfloat16)
    grad_query = (
        jnp.einsum("lhqk,lkhd->lqhd", grad_scores, key, preferred_element_type=jnp.float32) * 0.125
    )
    grad_key = (
        jnp.einsum("lhqk,lqhd->lkhd", grad_scores, query, preferred_element_type=jnp.float32)
        * 0.125
    )
    return (
        grad_query.astype(jnp.bfloat16),
        grad_key.astype(jnp.bfloat16),
        grad_value.astype(jnp.bfloat16),
    )


def on_device(
    latent_tokens, cond, w_ada, b_ada, w_qkv, b_qv, w_o, b_o, w_1, b_1, w_2, b_2, grad_out
):
    count, length, width = latent_tokens.shape
    head_size = width // HEADS
    per_block = math.gcd(count, max(1, 512 // length))
    blocks = count // per_block
    whole = (
        lax.all_gather(w_ada, "shard", axis=0, tiled=True),
        lax.all_gather(b_ada, "shard", axis=0, tiled=True),
        lax.all_gather(w_qkv, "shard", axis=0, tiled=True),
        lax.all_gather(b_qv, "shard", axis=0, tiled=True),
        lax.all_gather(w_o, "shard", axis=0, tiled=True),
        lax.all_gather(b_o, "shard", axis=0, tiled=True),
        lax.all_gather(w_1, "shard", axis=0, tiled=True),
        lax.all_gather(b_1, "shard", axis=0, tiled=True),
        lax.all_gather(w_2, "shard", axis=0, tiled=True),
        lax.all_gather(b_2, "shard", axis=0, tiled=True),
    )
    f_ada, f_bada, f_qkv, f_bqv, f_wo, f_bo, f_w1, f_b1, f_w2, f_b2 = whole
    tokens = latent_tokens.astype(jnp.float32)
    condition = cond.astype(jnp.float32)
    cs = jax.nn.silu(condition).astype(jnp.bfloat16)
    ada = jnp.dot(cs, f_ada, preferred_element_type=jnp.float32) + f_bada.astype(jnp.float32)
    shift1, scale1, gate1, shift2, scale2, gate2 = jnp.split(ada, 6, axis=-1)
    n1, rstd1 = layer_norm(tokens)
    m1 = (n1 * (1.0 + scale1[:, None]) + shift1[:, None]).astype(jnp.bfloat16)
    qkv = project(m1, f_qkv)
    bias_qv = f_bqv.astype(jnp.float32)
    query = (qkv[..., :width] + bias_qv[:width]).astype(jnp.bfloat16)
    key = qkv[..., width : 2 * width].astype(jnp.bfloat16)
    value = (qkv[..., 2 * width :] + bias_qv[width:]).astype(jnp.bfloat16)
    shape_blocks = (blocks, per_block, length, HEADS, head_size)
    q_blocks = query.reshape(shape_blocks)
    k_blocks = key.reshape(shape_blocks)
    v_blocks = value.reshape(shape_blocks)
    att_blocks, logsum = lax.map(attend, (q_blocks, k_blocks, v_blocks))
    attended = att_blocks.reshape(count, length, width)
    branch = project(attended, f_wo) + f_bo.astype(jnp.float32)
    x1 = tokens + gate1[:, None] * branch
    n2, rstd2 = layer_norm(x1)
    m2 = (n2 * (1.0 + scale2[:, None]) + shift2[:, None]).astype(jnp.bfloat16)
    hidden = project(m2, f_w1) + f_b1.astype(jnp.float32)
    gelu_out, gelu_vjp = jax.vjp(lambda t: jax.nn.gelu(t, approximate=True), hidden)
    gelu_low = gelu_out.astype(jnp.bfloat16)
    ffn = project(gelu_low, f_w2) + f_b2.astype(jnp.float32)
    block_out = (x1 + gate2[:, None] * ffn).astype(jnp.bfloat16)
    again = (
        lax.all_gather(w_ada, "shard", axis=0, tiled=True),
        lax.all_gather(w_qkv, "shard", axis=0, tiled=True),
        lax.all_gather(w_o, "shard", axis=0, tiled=True),
        lax.all_gather(w_1, "shard", axis=0, tiled=True),
        lax.all_gather(w_2, "shard", axis=0, tiled=True),
    )
    g_ada, g_qkv, g_wo, g_w1, g_w2 = again
    cotangent = grad_out.astype(jnp.float32)
    grad_ffn = (cotangent * gate2[:, None]).astype(jnp.bfloat16)
    d_gate2 = jnp.sum(cotangent * ffn, axis=1)
    gw_2 = weight_grad(gelu_low, grad_ffn)
    gb_2 = jnp.sum(grad_ffn.astype(jnp.float32), axis=(0, 1))
    grad_gelu = jnp.einsum("lse,de->lsd", grad_ffn, g_w2, preferred_element_type=jnp.float32)
    grad_hidden = gelu_vjp(grad_gelu)[0].astype(jnp.bfloat16)
    gw_1 = weight_grad(m2, grad_hidden)
    gb_1 = jnp.sum(grad_hidden.astype(jnp.float32), axis=(0, 1))
    grad_m2 = jnp.einsum("lse,de->lsd", grad_hidden, g_w1, preferred_element_type=jnp.float32)
    d_scale2 = jnp.sum(grad_m2 * n2, axis=1)
    d_shift2 = jnp.sum(grad_m2, axis=1)
    grad_x1 = cotangent + norm_back(n2, rstd2, grad_m2 * (1.0 + scale2[:, None]))
    grad_branch = (grad_x1 * gate1[:, None]).astype(jnp.bfloat16)
    d_gate1 = jnp.sum(grad_x1 * branch, axis=1)
    gw_o = weight_grad(attended, grad_branch)
    gb_o = jnp.sum(grad_branch.astype(jnp.float32), axis=(0, 1))
    grad_att = jnp.einsum(
        "lse,de->lsd", grad_branch, g_wo, preferred_element_type=jnp.float32
    ).astype(jnp.bfloat16)
    dq, dk, dv = lax.map(
        attend_back, (q_blocks, k_blocks, v_blocks, logsum, grad_att.reshape(shape_blocks))
    )
    grad_qkv = jnp.concatenate(
        [
            dq.reshape(count, length, width),
            dk.reshape(count, length, width),
            dv.reshape(count, length, width),
        ],
        axis=-1,
    )
    gw_qkv = weight_grad(m1, grad_qkv)
    column_sums = jnp.sum(grad_qkv.astype(jnp.float32), axis=(0, 1))
    gb_qv = jnp.concatenate([column_sums[:width], column_sums[2 * width :]])
    grad_m1 = jnp.einsum("lse,de->lsd", grad_qkv, g_qkv, preferred_element_type=jnp.float32)
    d_scale1 = jnp.sum(grad_m1 * n1, axis=1)
    d_shift1 = jnp.sum(grad_m1, axis=1)
    grad_tokens = grad_x1 + norm_back(n1, rstd1, grad_m1 * (1.0 + scale1[:, None]))
    grad_ada = jnp.concatenate(
        [d_shift1, d_scale1, d_gate1, d_shift2, d_scale2, d_gate2], axis=-1
    ).astype(jnp.bfloat16)
    gw_ada = jnp.dot(cs.T, grad_ada, preferred_element_type=jnp.float32)
    gb_ada = jnp.sum(grad_ada.astype(jnp.float32), axis=0)
    grad_cs = jnp.dot(grad_ada, g_ada.T, preferred_element_type=jnp.float32)
    silu_grad = jax.vjp(jax.nn.silu, condition)[1](grad_cs)[0]
    partial_value = (
        lax.psum_scatter(
            gw_ada.astype(jnp.bfloat16), "shard", scatter_dimension=0, tiled=True
        ).astype(jnp.float32),
        lax.psum_scatter(
            gb_ada.astype(jnp.bfloat16), "shard", scatter_dimension=0, tiled=True
        ).astype(jnp.float32),
        lax.psum_scatter(
            gw_qkv.astype(jnp.bfloat16), "shard", scatter_dimension=0, tiled=True
        ).astype(jnp.float32),
        lax.psum_scatter(
            gb_qv.astype(jnp.bfloat16), "shard", scatter_dimension=0, tiled=True
        ).astype(jnp.float32),
        lax.psum_scatter(
            gw_o.astype(jnp.bfloat16), "shard", scatter_dimension=0, tiled=True
        ).astype(jnp.float32),
        lax.psum_scatter(
            gb_o.astype(jnp.bfloat16), "shard", scatter_dimension=0, tiled=True
        ).astype(jnp.float32),
        lax.psum_scatter(
            gw_1.astype(jnp.bfloat16), "shard", scatter_dimension=0, tiled=True
        ).astype(jnp.float32),
        lax.psum_scatter(
            gb_1.astype(jnp.bfloat16), "shard", scatter_dimension=0, tiled=True
        ).astype(jnp.float32),
        lax.psum_scatter(
            gw_2.astype(jnp.bfloat16), "shard", scatter_dimension=0, tiled=True
        ).astype(jnp.float32),
        lax.psum_scatter(
            gb_2.astype(jnp.bfloat16), "shard", scatter_dimension=0, tiled=True
        ).astype(jnp.float32),
    )
    summed = (
        lax.psum(partial_value[0].astype(jnp.bfloat16), "rep").astype(jnp.float32),
        lax.psum(partial_value[1].astype(jnp.bfloat16), "rep").astype(jnp.float32),
        lax.psum(partial_value[2].astype(jnp.bfloat16), "rep").astype(jnp.float32),
        lax.psum(partial_value[3].astype(jnp.bfloat16), "rep").astype(jnp.float32),
        lax.psum(partial_value[4].astype(jnp.bfloat16), "rep").astype(jnp.float32),
        lax.psum(partial_value[5].astype(jnp.bfloat16), "rep").astype(jnp.float32),
        lax.psum(partial_value[6].astype(jnp.bfloat16), "rep").astype(jnp.float32),
        lax.psum(partial_value[7].astype(jnp.bfloat16), "rep").astype(jnp.float32),
        lax.psum(partial_value[8].astype(jnp.bfloat16), "rep").astype(jnp.float32),
        lax.psum(partial_value[9].astype(jnp.bfloat16), "rep").astype(jnp.float32),
    )
    return (
        block_out,
        grad_tokens,
        silu_grad,
        summed[0],
        summed[1],
        summed[2],
        summed[3],
        summed[4],
        summed[5],
        summed[6],
        summed[7],
        summed[8],
        summed[9],
    )


def solution(mesh):
    in_specs = (
        P(("rep", "shard"), None, None),
        P(("rep", "shard"), None),
        P("shard", None),
        P("shard"),
        P("shard", None),
        P("shard"),
        P("shard", None),
        P("shard"),
        P("shard", None),
        P("shard"),
        P("shard", None),
        P("shard"),
        P(("rep", "shard"), None, None),
    )
    out_specs = (
        P(("rep", "shard"), None, None),
        P(("rep", "shard"), None, None),
        P(("rep", "shard"), None),
        P("shard", None),
        P("shard"),
        P("shard", None),
        P("shard"),
        P("shard", None),
        P("shard"),
        P("shard", None),
        P("shard"),
        P("shard", None),
        P("shard"),
    )
    return jax.shard_map(
        on_device, mesh=mesh, in_specs=in_specs, out_specs=out_specs, check_vma=False
    )
```

profile of v0, /device:TPU:0, one launch (start us, length us, event | category | flops | bytes accessed | tf_op | source)
XLA Modules:
  0.0 425.0 jit_solution(18000375624998559178)
XLA Ops:
  13.5 6.1 %all-gather = bf16[4,1,384]{2,1,0:T(2,128)(2,1)S(1)} all-gather(bf16[1,1,384]{2,1,0:T(2,128)(2,1)S(1)} %reshape.148), channel_id=1, replica_groups=mesh['rep'=8,'shard'=4] {'shard'}, dimensions={0}, use_global_device_ids=true | all-gather | bytes 3840 | tf_op jit(solution)/shard_map/all_gather | solution.py:81
  23.6 12.3 %all-reduce.12 = (bf16[2304]{0:T(1024)(128)(2,1)S(1)}, bf16[768]{0:T(1024)(128)(2,1)S(1)}, bf16[384]{0:T(512)(128)(2,1)S(1)}, bf16[384]{0:T(512)(128)(2,1)S(1)}) all-reduce(bf16[2304]{0:T(1024)(128)(2,1)S(1)} %dynamic-update-slice, bf16[768]{0:T(1024)(128)(2,1)S(1)} %dynamic-update-slice.1, ...), channel_id=1, replica_groups=mesh['rep'=8,'shard'=4] {'shard'}, use_global_device_ids=true, to_apply=%add | all-reduce | flops 3840 | bytes 15360
  39.2 5.9 %all_gather.39 = bf16[384,384]{1,0:T(8,128)(2,1)S(1)} all-gather(bf16[96,384]{1,0:T(8,128)(2,1)S(1)} %copy-done.16), channel_id=1, replica_groups=mesh['rep'=8,'shard'=4] {'shard'}, dimensions={0}, use_global_device_ids=true | all-gather | bytes 368640 | tf_op jit(solution)/shard_map/all_gather | solution.py:78
  45.1 11.3 %all_gather.37 = bf16[384,1152]{1,0:T(8,128)(2,1)S(1)} all-gather(bf16[96,1152]{1,0:T(8,128)(2,1)S(1)} %copy-done.15), channel_id=1, replica_groups=mesh['rep'=8,'shard'=4] {'shard'}, dimensions={0}, use_global_device_ids=true | all-gather | bytes 1105920 | tf_op jit(solution)/shard_map/all_gather | solution.py:76
  74.2 18.9 %while.26 = (s32[]{:T(128)}, bf16[4,2,256,6,64]{2,4,3,1,0:T(8,128)(2,1)}, f32[4,2,6,256,1]{3,2,1,4,0:T(8,128)S(1)}, bf16[4,2,256,6,64]{2,4,3,1,0:T(8,128)(2,1)},...) while((s32[]{:T(128)}, ...), condition=%wide.region_5.6_spmd, body=%wide.region_2.5_spmd.sunk | while | flops 208598016 | bytes 11122777 | solution.py:102
  93.1 4.6 %fusion.115 = (f32[8,256]{1,0:T(8,128)S(1)}, f32[8,256,384]{2,1,0:T(8,128)S(1)}, f32[8,256,384]{2,1,0:T(8,128)}) fusion(f32[384]{0:T(512)S(1)} %convert_element_type.177, f32[8,384]{1,0:T(8,128)S(1)} %get-tuple-element.197, bf16[8,256,384]{2,1,0:T(8,128)(2,1)S(1)} %copy-done, bf16[8,256,384]{1,2,0:T(8,128)(2,1)} %bitcast.178, ...), kind=kOutput, calls=%fused_computation.164 | convolution fusion | flops 607909888 | bytes 9754112 | tf_op jit(solution)/shard_map/lsd,de->lse/dot_general | solution.py:23
  100.7 11.0 %multiply_convert_fusion.1 = (bf16[8,256,1536]{2,1,0:T(8,128)(2,1)}, f32[8,256,1536]{2,1,0:T(8,128)}) fusion(f32[1536]{0:T(1024)} %reshape.150, bf16[384,1536]{1,0:T(8,128)(2,1)} %all-gather.7.cloned.1.call-done, f32[8,256,384]{2,1,0:T(8,128)} %copy-done.1, f32[8,384]{1,0:T(8,128)} %get-tuple-element.193, f32[8,384]{1,0:T(8,128)} %get-tuple-element.194, ...), kind=kOutput, calls=%fused_computation.69 | convolution fusion | flops 2451308544 | bytes 23246848 | tf_op jit(solution)/shard_map/lsd,de->lse/dot_general | solution.py:23
  111.7 15.0 %fusion.120 = (bf16[1536]{0:T(1024)(128)(2,1)}, bf16[8,256,1536]{2,1,0:T(8,128)(2,1)S(1)}) fusion(f32[8,256,1536]{2,1,0:T(8,128)} %get-tuple-element.206, f32[1536]{0:T(1024)} %reshape.150, bf16[1536,384]{1,0:T(8,128)(2,1)} %all-gather.9.cloned.1.call-done, bf16[8,256,384]{2,1,0:T(8,128)(2,1)} %param.29, f32[8,384]{1,0:T(8,128)} %get-tuple-element.192), kind=kOutput, calls=%fused_computation.169 | convolution fusion | flops 2487482880 | bytes 21648384 | tf_op jit(solution)/shard_map/lse,de->lsd/dot_general | solution.py:126
  126.9 3.6 fusion.92
  133.7 6.0 %fusion.79 = (bf16[8,384]{1,0:T(8,128)(2,1)}, bf16[8,256,384]{2,1,0:T(8,128)(2,1)}, bf16[8,384]{1,0:T(8,128)(2,1)}, f32[8,256]{1,0:T(8,128)S(1)}, f32[8,256]{1,0:T(8,128)S(1)}, /*index=5*/bf16[8,384]{1,0:T(8,128)(2,1)}) fusion(bf16[8,256,384]{2,1,0:T(8,128)(2,1)S(1)} %copy-done.13, f32[384]{0:T(512)S(1)} %copy-done.36, f32[8,256,384]{2,1,0:T(8,128)S(1)} %copy-done.2, ...), kind=kOutput, calls=%fused_computation.94 | convolution fusion | flops 2428488704 | bytes 16985600 | tf_op jit(solution)/shard_map/lsd,de->lse/dot_general | solution.py:23
  139.7 4.1 fusion.114
  146.6 3.7 convolution_convert_fusion.1
  157.0 37.3 %while.27 = (s32[]{:T(128)}, bf16[4,2,256,6,64]{2,4,3,1,0:T(8,128)(2,1)}, bf16[4,2,256,6,64]{2,4,3,1,0:T(8,128)(2,1)}, bf16[4,2,256,6,64]{2,4,3,1,0:T(8,128)(2,1...) while((s32[]{:T(128)}, ...), condition=%wide.region_12.13_spmd, body=%wide.region_10.12_spmd.sunk | while | flops 513733632 | bytes 33916044 | solution.py:141
  201.3 6.2 %fusion.82 = bf16[384,1152]{1,0:T(8,128)(2,1)} fusion(bf16[8,256,384]{2,1,0:T(8,128)(2,1)S(1)} %copy-done, f32[8,384]{1,0:T(8,128)S(1)} %copy-done.24, f32[8,384]{1,0:T(8,128)S(1)} %get-tuple-element.196, f32[8,256]{1,0:T(8,128)S(1)} %add_rsqrt_fusion.1, f32[8,256]{1,0:T(8,128)S(1)} %broadcast_multiply_fusion.5, bf16[8,256,384]{2,1,0:T(8,128)(2,1)} %copy.85, ...), kind=kOutput, calls=%fused_computation.111 | convolution fusion | flops 1831256064 | bytes 7217152 | tf_op jit(solution)/shard_map/lsd,lse->de/dot_general | solution.py:27
  207.6 7.6 %fusion.83 = bf16[384,1536]{1,0:T(8,128)(2,1)} fusion(bf16[8,256,1536]{2,1,0:T(8,128)(2,1)} %copy-done.39, f32[8,256,384]{2,1,0:T(8,128)} %copy-done.1, f32[8,384]{1,0:T(8,128)S(1)} %copy-done.29, f32[8,384]{1,0:T(8,128)S(1)} %copy-done.22, f32[8,256]{1,0:T(8,128)S(1)} %copy-done.26, f32[8,256]{1,0:T(8,128)S(1)} %broadcast_multiply_fusion.4), kind=kOutput, calls=%fused_computation.112 | convolution fusion | flops 2420441088 | bytes 10657792 | tf_op jit(solution)/shard_map/lsd,lse->de/dot_general | solution.py:27
  215.5 8.0 %fusion.84 = bf16[1536,384]{1,0:T(8,128)(2,1)} fusion(bf16[8,256,1536]{2,1,0:T(8,128)(2,1)} %get-tuple-element.205, bf16[8,256,384]{2,1,0:T(8,128)(2,1)} %param.29, f32[8,384]{1,0:T(8,128)S(1)} %copy-done.20), kind=kOutput, calls=%fused_computation.113 | convolution fusion | flops 2418868224 | bytes 9056256 | tf_op jit(solution)/shard_map/lsd,lse->de/dot_general | solution.py:27
  223.6 6.2 %fusion.76 = (bf16[8,384]{1,0:T(8,128)(2,1)S(1)}, f32[8,256]{1,0:T(8,128)S(1)}, f32[8,256]{1,0:T(8,128)S(1)}, bf16[8,384]{1,0:T(8,128)(2,1)S(1)}, f32[8,256,384]{2,1,0:T(8,128)S(1)}) fusion(bf16[8,256,384]{2,1,0:T(8,128)(2,1)S(1)} %copy-done, f32[8,256]{1,0:T(8,128)S(1)} %add_rsqrt_fusion.1, f32[8,256]{1,0:T(8,128)S(1)} %broadcast_multiply_fusion.5, ...), kind=kOutput, calls=%fused_computation.91 | convolution fusion | flops 1833949184 | bytes 10379264 | tf_op jit(solution)/shard_map/lse,de->lsd/dot_general | solution.py:155
  229.9 3.1 multiply_reduce_fusion.3
  235.2 24.6 %reduce-scatter.12.cloned.1.call-done = bf16[96,1536]{1,0:T(8,128)(2,1)} async-done(((bf16[384,1536]{1,0:T(8,128)(2,1)}), bf16[96,1536]{1,0:T(8,128)(2,1)}) %reduce-scatter.12.cloned.1.call-update) | async-done | bytes 294928 | tf_op jit(solution)/shard_map/reduce_scatter | solution.py:185
  259.8 28.5 %reduce-scatter.14.cloned.1.call-done = bf16[384,384]{1,0:T(8,128)(2,1)} async-done(((bf16[1536,384]{1,0:T(8,128)(2,1)}), bf16[384,384]{1,0:T(8,128)(2,1)}) %reduce-scatter.14.cloned.1.call-update) | async-done | bytes 294928 | tf_op jit(solution)/shard_map/reduce_scatter | solution.py:191
  288.3 32.0 %reduce-scatter.6.cloned.1.call-done = bf16[96,2304]{1,0:T(8,128)(2,1)} async-done(((bf16[384,2304]{1,0:T(8,128)(2,1)}), bf16[96,2304]{1,0:T(8,128)(2,1)}) %reduce-scatter.6.cloned.1.call-update) | async-done | bytes 442384 | tf_op jit(solution)/shard_map/reduce_scatter | solution.py:167
  325.2 10.5 %all-reduce.11 = (bf16[2304]{0:T(1024)(128)(2,1)S(1)}, bf16[768]{0:T(1024)(128)(2,1)S(1)}, bf16[384]{0:T(512)(128)(2,1)S(1)}, bf16[1536]{0:T(1024)(128)(2,1)S(1)}, bf16[384]{0:T(512)(128)(2,1)S(1)}) all-reduce(bf16[2304]{0:T(1024)(128)(2,1)S(1)} %reduce_sum.215, ...), channel_id=3, replica_groups=mesh['rep'=8,'shard'=4] {'shard'}, use_global_device_ids=true, to_apply=%region_24.25.clone | all-reduce | flops 5376 | bytes 21504
  336.1 22.2 %all-reduce.9 = (bf16[576]{0:T(1024)(128)(2,1)S(1)}, bf16[192]{0:T(256)(128)(2,1)S(1)}, bf16[96]{0:T(256)(128)(2,1)S(1)}, bf16[384]{0:T(512)(128)(2,1)S(1)}, bf16[96]{0:T(256)(128)(2,1)S(1)}) all-reduce(bf16[576]{0:T(1024)(128)(2,1)S(1)} %dynamic-slice.5, ...), channel_id=1, replica_groups=mesh['rep'=8,'shard'=4] {'rep'}, use_global_device_ids=true, to_apply=%region_25.26 | all-reduce | flops 1344 | bytes 5376 | tf_op jit(solution)/shard_map/psum | solution.py:200
  362.3 47.9 %all-reduce.15.cloned.1.call-done = (bf16[96,2304]{1,0:T(8,128)(2,1)}, bf16[96,1152]{1,0:T(8,128)(2,1)}, bf16[96,384]{1,0:T(8,128)(2,1)}, bf16[96,1536]{1,0:T(8,128)(2,1)}, bf16[384,384]{1,0:T(8,128)(2,1)}) async-done(((bf16[96,2304]{1,0:T(8,128)(2,1)}, bf16[96,1152]{1,0:T(8,128)(2,1)}, bf16[96,384]{1,0:T(8,128)(2,1)}, bf16[96,1536]{1,0:T(8,128)(2,1)}, bf16[384,384]{1,0:T(8,128)(2,1)}), ...) | async-done | bytes 1327120 | tf_op jit(solution)/shard_map/psum | solution.py:199
  (226 shorter events, 125.1 us)
Async XLA Ops:
  7.2 31.1 %copy-start = (bf16[8,256,384]{2,1,0:T(8,128)(2,1)S(1)}, bf16[8,256,384]{2,1,0:T(8,128)(2,1)}, u32[]{:S(2)}) copy-start(bf16[8,256,384]{2,1,0:T(8,128)(2,1)} %param.17) | copy-start | bytes 4718596
  7.2 32.0 %copy-start.16 = (bf16[96,384]{1,0:T(8,128)(2,1)S(1)}, bf16[96,384]{1,0:T(8,128)(2,1)}, u32[]{:S(2)}) copy-start(bf16[96,384]{1,0:T(8,128)(2,1)} %param.23) | copy-start | bytes 221188
  7.2 37.9 %copy-start.15 = (bf16[96,1152]{1,0:T(8,128)(2,1)S(1)}, bf16[96,1152]{1,0:T(8,128)(2,1)}, u32[]{:S(2)}) copy-start(bf16[96,1152]{1,0:T(8,128)(2,1)} %param.21) | copy-start | bytes 663556
  7.2 49.2 %copy-start.17 = (bf16[8,384]{1,0:T(8,128)(2,1)S(1)}, bf16[8,384]{1,0:T(8,128)(2,1)}, u32[]{:S(2)}) copy-start(bf16[8,384]{1,0:T(8,128)(2,1)} %param.18) | copy-start | bytes 18436
  7.2 49.2 %all-gather.5.cloned.1.call-start = ((), (), s32[]{:S(2)}) async-start(), calls=%async_computation.5 | async-start | bytes 2211840 | tf_op jit(solution)/shard_map/all_gather | solution.py:74
  8.0 92.7 %all-gather.7.cloned.1.call-start = ((), (), s32[]{:S(2)}) async-start(), calls=%async_computation.6 | async-start | bytes 1474560 | tf_op jit(solution)/shard_map/all_gather | solution.py:80
  8.7 103.0 %all-gather.9.cloned.1.call-start = ((), (), s32[]{:S(2)}) async-start(), calls=%async_computation.7 | async-start | bytes 1474560 | tf_op jit(solution)/shard_map/all_gather | solution.py:82
  9.4 225.7 %reduce-scatter.10.cloned.1.call-start = ((), (), s32[]{:S(2)}) async-start(), calls=%async_computation.10 | async-start | bytes 368640 | tf_op jit(solution)/shard_map/reduce_scatter | solution.py:179
  35.9 57.2 %copy-start.27 = (f32[384]{0:T(512)}, f32[384]{0:T(512)S(1)}, u32[]{:S(2)}) copy-start(f32[384]{0:T(512)S(1)} %convert_element_type.177) | copy-start | bytes 4612
  111.7 15.1 %copy-start.38 = (bf16[384,1536]{1,0:T(8,128)(2,1)S(1)}, bf16[384,1536]{1,0:T(8,128)(2,1)}, u32[]{:S(2)}) copy-start(bf16[384,1536]{1,0:T(8,128)(2,1)} %all-gather.7.cloned.1.call-done) | copy-start | bytes 3538948
  126.8 6.8 %copy-start.40 = (bf16[8,256,1536]{2,1,0:T(8,128)(2,1)S(1)}, bf16[8,256,1536]{2,1,0:T(8,128)(2,1)}, u32[]{:S(2)}) copy-start(bf16[8,256,1536]{2,1,0:T(8,128)(2,1)} %get-tuple-element.205) | copy-start | bytes 18874372
  150.3 84.8 %reduce-scatter.8.cloned.1.call-start = ((), (), s32[]{:S(2)}) async-start(), calls=%async_computation.9 | async-start | bytes 1105920 | tf_op jit(solution)/shard_map/reduce_scatter | solution.py:173
  207.5 8.0 %copy-start.20 = (f32[8,384]{1,0:T(8,128)S(1)}, f32[8,384]{1,0:T(8,128)}, u32[]{:S(2)}) copy-start(f32[8,384]{1,0:T(8,128)} %get-tuple-element.192) | copy-start | bytes 36868
  207.5 52.3 %reduce-scatter.12.cloned.1.call-start = ((), (), s32[]{:S(2)}) async-start(), calls=%async_computation.11 | async-start | bytes 1474560 | tf_op jit(solution)/shard_map/reduce_scatter | solution.py:185
  215.2 8.3 %copy-start.10 = (bf16[8,256,384]{2,1,0:T(8,128)(2,1)S(1)}, bf16[8,256,384]{2,1,0:T(8,128)(2,1)}, u32[]{:S(2)}) copy-start(bf16[8,256,384]{2,1,0:T(8,128)(2,1)} %copy.85) | copy-start | bytes 4718596
  215.2 73.0 %reduce-scatter.14.cloned.1.call-start = ((), (), s32[]{:S(2)}) async-start(), calls=%async_computation.12 | async-start | bytes 1474560 | tf_op jit(solution)/shard_map/reduce_scatter | solution.py:191
  223.5 96.8 %reduce-scatter.6.cloned.1.call-start = ((), (), s32[]{:S(2)}) async-start(), calls=%async_computation.8 | async-start | bytes 2211840 | tf_op jit(solution)/shard_map/reduce_scatter | solution.py:167
  233.0 89.9 %copy-start.11 = (bf16[8,256,384]{2,1,0:T(8,128)(2,1)S(1)}, bf16[8,256,384]{2,1,0:T(8,128)(2,1)}, u32[]{:S(2)}) copy-start(bf16[8,256,384]{2,1,0:T(8,128)(2,1)} %copy.85) | copy-start | bytes 4718596
  235.0 90.2 %copy-start.33 = (bf16[384]{0:T(512)(128)(2,1)S(1)}, bf16[384]{0:T(512)(128)(2,1)}, u32[]{:S(2)}) copy-start(bf16[384]{0:T(512)(128)(2,1)} %get-tuple-element.172) | copy-start | bytes 2308
  235.0 90.2 %copy-start.34 = (bf16[384]{0:T(512)(128)(2,1)S(1)}, bf16[384]{0:T(512)(128)(2,1)}, u32[]{:S(2)}) copy-start(bf16[384]{0:T(512)(128)(2,1)} %get-tuple-element.191) | copy-start | bytes 2308
  235.0 90.2 %copy-start.35 = (bf16[1536]{0:T(1024)(128)(2,1)S(1)}, bf16[1536]{0:T(1024)(128)(2,1)}, u32[]{:S(2)}) copy-start(bf16[1536]{0:T(1024)(128)(2,1)} %get-tuple-element.208) | copy-start | bytes 9220
  235.0 126.1 %copy-start.6 = (bf16[384,2304]{1,0:T(8,128)(2,1)S(1)}, bf16[384,2304]{1,0:T(8,128)(2,1)}, u32[]{:S(2)}) copy-start(bf16[384,2304]{1,0:T(8,128)(2,1)} %all-gather.5.cloned.1.call-done) | copy-start | bytes 5308420
  235.1 175.2 %all-reduce.15.cloned.1.call-start = ((), (), s32[]{:S(2)}) async-start(), calls=%async_computation.13 | async-start | bytes 2654208 | tf_op jit(solution)/shard_map/psum | solution.py:199
  410.2 7.1 %copy-start.14 = (bf16[384,384]{1,0:T(8,128)(2,1)S(1)}, bf16[384,384]{1,0:T(8,128)(2,1)}, u32[]{:S(2)}) copy-start(bf16[384,384]{1,0:T(8,128)(2,1)} %get-tuple-element.162) | copy-start | bytes 884740
  (29 other events, 119.7 us)
Sparse Core Ops, SparseCore 0:
  9.6 23.5 all-gather.4
  34.8 19.2 all-gather.6
  55.6 17.1 all-gather.8
  150.4 20.4 reduce-scatter.9
  207.6 23.9 reduce-scatter.7
  234.0 25.7 reduce-scatter.11
  262.5 25.7 reduce-scatter.13
  290.9 29.3 reduce-scatter.5
  324.8 85.3 all-reduce.14
where the time goes:
time: 429 us; the launch traced here: 425 us
  waiting for transfers between devices  135 us (31%)
  matrix products  133 us (31%)
  blocking collectives  68.3 us (16%)
  local copies, waits for them, and re-layouts  35.9 us (8%)
  other arithmetic  33 us (8%)
  between operations  19.2 us (4%)
    psum x1, waiting for transfers between devices, on_device(): lax.psum(partial_value[0].astype(jnp.bfloat16), 'rep').astype(jnp.float32)  47.9 us
    reduce_scatter x1, waiting for transfers between devices, on_device(): lax.psum_scatter(gw_ada.astype(jnp.bfloat16), 'shard', scatter_dimension=...  32 us
    reduce_scatter x1, waiting for transfers between devices, on_device(): lax.psum_scatter(gw_2.astype(jnp.bfloat16), 'shard', scatter_dimension=0,...  28.5 us
    dot_general x4, matrix products, project(): jnp.einsum('lsd,de->lse', left, right, preferred_element_type=jnp.float32)  24.6 us
    reduce_scatter x1, waiting for transfers between devices, on_device(): lax.psum_scatter(gw_1.astype(jnp.bfloat16), 'shard', scatter_dimension=0,...  24.6 us
    dot_general x4, matrix products, weight_grad(): jnp.einsum('lsd,lse->de', left, right, preferred_element_type=jnp.float32)  23.4 us
    unnamed x2, blocking collectives  22.9 us
    psum x1, blocking collectives, on_device(): lax.psum(partial_value[1].astype(jnp.bfloat16), 'rep').astype(jnp.float32)  22.2 us
  transfers between devices with their start and end apart: 9, of which 4 were waited for; matrix products, arithmetic and copies ran while one was open for 36% of the time, Pallas kernels for 0%

commit v1 on v0

--- a/solution.py
+++ b/solution.py
@@ -197,7 +197,9 @@
     )
     summed = (
         lax.psum(partial_value[0].astype(jnp.bfloat16), "rep").astype(jnp.float32),
-        lax.psum(partial_value[1].astype(jnp.bfloat16), "rep").astype(jnp.float32),
+        jnp.sum(lax.all_gather(partial_value[1].astype(jnp.bfloat16), "rep"), axis=0).astype(
+            jnp.float32
+        ),
         lax.psum(partial_value[2].astype(jnp.bfloat16), "rep").astype(jnp.float32),
         lax.psum(partial_value[3].astype(jnp.bfloat16), "rep").astype(jnp.float32),
         lax.psum(partial_value[4].astype(jnp.bfloat16), "rep").astype(jnp.float32),

time: 429 us -> 429 us (level)
  waiting for transfers between devices: 135 us -> 118 us
  blocking collectives: 68.3 us -> 83.4 us
    unnamed x2 -> x3, blocking collectives: 22.9 us -> 60.2 us
    psum x1 -> x0, blocking collectives: 22.2 us -> none  [on_device(): lax.psum(partial_value[1].astype(jnp.bfloat16), 'rep').astype(jnp.float32)]
    psum x1, waiting for transfers between devices: 47.9 us -> 30.5 us  [on_device(): lax.psum(partial_value[0].astype(jnp.bfloat16), 'rep').astype(jnp.float32)]
    unnamed x100 -> x103, local copies, waits for them, and re-layouts: 12 us -> 12.8 us
where the time goes in v1:
time: 429 us; the launch traced here: 425 us
  matrix products  133 us (31%)
  waiting for transfers between devices  118 us (28%)
  blocking collectives  83.4 us (19%)
  local copies, waits for them, and re-layouts  36.8 us (9%)
  other arithmetic  33.5 us (8%)
  between operations  19.8 us (5%)
    unnamed x3, blocking collectives  60.2 us
    reduce_scatter x1, waiting for transfers between devices, on_device(): lax.psum_scatter(gw_ada.astype(jnp.bfloat16), 'shard', scatter_dimension=...  32 us
    psum x1, waiting for transfers between devices, on_device(): lax.psum(partial_value[0].astype(jnp.bfloat16), 'rep').astype(jnp.float32)  30.5 us
    reduce_scatter x1, waiting for transfers between devices, on_device(): lax.psum_scatter(gw_2.astype(jnp.bfloat16), 'shard', scatter_dimension=0,...  28.5 us
    dot_general x4, matrix products, project(): jnp.einsum('lsd,de->lse', left, right, preferred_element_type=jnp.float32)  24.6 us
    reduce_scatter x1, waiting for transfers between devices, on_device(): lax.psum_scatter(gw_1.astype(jnp.bfloat16), 'shard', scatter_dimension=0,...  24.6 us
    dot_general x4, matrix products, weight_grad(): jnp.einsum('lsd,lse->de', left, right, preferred_element_type=jnp.float32)  23.4 us
    dot_general x1, matrix products, on_device(): jnp.einsum('lse,de->lsd', grad_ffn, g_w2, preferred_element_type=jnp.floa...  15 us
  transfers between devices with their start and end apart: 9, of which 4 were waited for; matrix products, arithmetic and copies ran while one was open for 36% of the time, Pallas kernels for 0%

profile of v1, /device:TPU:0, one launch (start us, length us, event | category | flops | bytes accessed | tf_op | source)
XLA Modules:
  0.0 424.7 jit_solution(16692935804969683687)
XLA Ops:
  13.5 6.1 %all-gather.1 = bf16[4,1,384]{2,1,0:T(2,128)(2,1)S(1)} all-gather(bf16[1,1,384]{2,1,0:T(2,128)(2,1)S(1)} %reshape.152), channel_id=1, replica_groups=mesh['rep'=8,'shard'=4] {'shard'}, dimensions={0}, use_global_device_ids=true | all-gather | bytes 3840 | tf_op jit(solution)/shard_map/all_gather | solution.py:81
  23.6 12.3 %all-reduce.13 = (bf16[2304]{0:T(1024)(128)(2,1)S(1)}, bf16[768]{0:T(1024)(128)(2,1)S(1)}, bf16[384]{0:T(512)(128)(2,1)S(1)}, bf16[384]{0:T(512)(128)(2,1)S(1)}) all-reduce(bf16[2304]{0:T(1024)(128)(2,1)S(1)} %dynamic-update-slice, bf16[768]{0:T(1024)(128)(2,1)S(1)} %dynamic-update-slice.1, ...), channel_id=1, replica_groups=mesh['rep'=8,'shard'=4] {'shard'}, use_global_device_ids=true, to_apply=%add | all-reduce | flops 3840 | bytes 15360
  39.2 5.9 %all_gather.45 = bf16[384,384]{1,0:T(8,128)(2,1)S(1)} all-gather(bf16[96,384]{1,0:T(8,128)(2,1)S(1)} %copy-done.15), channel_id=1, replica_groups=mesh['rep'=8,'shard'=4] {'shard'}, dimensions={0}, use_global_device_ids=true | all-gather | bytes 368640 | tf_op jit(solution)/shard_map/all_gather | solution.py:78
  45.1 11.3 %all_gather.43 = bf16[384,1152]{1,0:T(8,128)(2,1)S(1)} all-gather(bf16[96,1152]{1,0:T(8,128)(2,1)S(1)} %copy-done.14), channel_id=1, replica_groups=mesh['rep'=8,'shard'=4] {'shard'}, dimensions={0}, use_global_device_ids=true | all-gather | bytes 1105920 | tf_op jit(solution)/shard_map/all_gather | solution.py:76
  74.2 18.9 %while.26 = (s32[]{:T(128)}, bf16[4,2,256,6,64]{2,4,3,1,0:T(8,128)(2,1)}, f32[4,2,6,256,1]{3,2,1,4,0:T(8,128)S(1)}, bf16[4,2,256,6,64]{2,4,3,1,0:T(8,128)(2,1)},...) while((s32[]{:T(128)}, ...), condition=%wide.region_5.6_spmd, body=%wide.region_2.5_spmd.sunk | while | flops 208598016 | bytes 11122777 | solution.py:102
  93.1 4.6 %fusion.115 = (f32[8,256]{1,0:T(8,128)S(1)}, f32[8,256,384]{2,1,0:T(8,128)S(1)}, f32[8,256,384]{2,1,0:T(8,128)}) fusion(f32[384]{0:T(512)S(1)} %convert_element_type.179, f32[8,384]{1,0:T(8,128)S(1)} %get-tuple-element.197, bf16[8,256,384]{2,1,0:T(8,128)(2,1)S(1)} %copy-done, bf16[8,256,384]{1,2,0:T(8,128)(2,1)} %bitcast.179, ...), kind=kOutput, calls=%fused_computation.164 | convolution fusion | flops 607909888 | bytes 9754112 | tf_op jit(solution)/shard_map/lsd,de->lse/dot_general | solution.py:23
  100.7 11.0 %multiply_convert_fusion.1 = (bf16[8,256,1536]{2,1,0:T(8,128)(2,1)}, f32[8,256,1536]{2,1,0:T(8,128)}) fusion(f32[1536]{0:T(1024)} %reshape.154, bf16[384,1536]{1,0:T(8,128)(2,1)} %all-gather.8.cloned.1.call-done, f32[8,256,384]{2,1,0:T(8,128)} %copy-done.1, f32[8,384]{1,0:T(8,128)} %get-tuple-element.193, f32[8,384]{1,0:T(8,128)} %get-tuple-element.194, ...), kind=kOutput, calls=%fused_computation.69 | convolution fusion | flops 2451308544 | bytes 23246848 | tf_op jit(solution)/shard_map/lsd,de->lse/dot_general | solution.py:23
  111.7 15.0 %fusion.120 = (bf16[1536]{0:T(1024)(128)(2,1)}, bf16[8,256,1536]{2,1,0:T(8,128)(2,1)S(1)}) fusion(f32[8,256,1536]{2,1,0:T(8,128)} %get-tuple-element.206, f32[1536]{0:T(1024)} %reshape.154, bf16[1536,384]{1,0:T(8,128)(2,1)} %all-gather.10.cloned.1.call-done, bf16[8,256,384]{2,1,0:T(8,128)(2,1)} %param.29, f32[8,384]{1,0:T(8,128)} %get-tuple-element.192), kind=kOutput, calls=%fused_computation.169 | convolution fusion | flops 2487482880 | bytes 21648384 | tf_op jit(solution)/shard_map/lse,de->lsd/dot_general | solution.py:126
  126.9 3.6 fusion.92
  133.7 6.0 %fusion.79 = (bf16[8,384]{1,0:T(8,128)(2,1)}, bf16[8,256,384]{2,1,0:T(8,128)(2,1)}, bf16[8,384]{1,0:T(8,128)(2,1)}, f32[8,256]{1,0:T(8,128)S(1)}, f32[8,256]{1,0:T(8,128)S(1)}, /*index=5*/bf16[8,384]{1,0:T(8,128)(2,1)}) fusion(bf16[8,256,384]{2,1,0:T(8,128)(2,1)S(1)} %copy-done.12, f32[384]{0:T(512)S(1)} %copy-done.35, f32[8,256,384]{2,1,0:T(8,128)S(1)} %copy-done.2, ...), kind=kOutput, calls=%fused_computation.94 | convolution fusion | flops 2428488704 | bytes 16985600 | tf_op jit(solution)/shard_map/lsd,de->lse/dot_general | solution.py:23
  139.7 4.1 fusion.114
  146.6 3.7 convolution_convert_fusion.1
  157.0 37.3 %while.27 = (s32[]{:T(128)}, bf16[4,2,256,6,64]{2,4,3,1,0:T(8,128)(2,1)}, bf16[4,2,256,6,64]{2,4,3,1,0:T(8,128)(2,1)}, bf16[4,2,256,6,64]{2,4,3,1,0:T(8,128)(2,1...) while((s32[]{:T(128)}, ...), condition=%wide.region_12.13_spmd, body=%wide.region_10.12_spmd.sunk | while | flops 513733632 | bytes 33916044 | solution.py:141
  201.3 6.2 %fusion.82 = bf16[384,1152]{1,0:T(8,128)(2,1)} fusion(bf16[8,256,384]{2,1,0:T(8,128)(2,1)S(1)} %copy-done, f32[8,384]{1,0:T(8,128)S(1)} %copy-done.23, f32[8,384]{1,0:T(8,128)S(1)} %get-tuple-element.196, f32[8,256]{1,0:T(8,128)S(1)} %add_rsqrt_fusion.1, f32[8,256]{1,0:T(8,128)S(1)} %broadcast_multiply_fusion.5, bf16[8,256,384]{2,1,0:T(8,128)(2,1)} %copy.85, ...), kind=kOutput, calls=%fused_computation.111 | convolution fusion | flops 1831256064 | bytes 7217152 | tf_op jit(solution)/shard_map/lsd,lse->de/dot_general | solution.py:27
  207.6 7.6 %fusion.83 = bf16[384,1536]{1,0:T(8,128)(2,1)} fusion(bf16[8,256,1536]{2,1,0:T(8,128)(2,1)} %copy-done.39, f32[8,256,384]{2,1,0:T(8,128)} %copy-done.1, f32[8,384]{1,0:T(8,128)S(1)} %copy-done.28, f32[8,384]{1,0:T(8,128)S(1)} %copy-done.21, f32[8,256]{1,0:T(8,128)S(1)} %copy-done.25, f32[8,256]{1,0:T(8,128)S(1)} %broadcast_multiply_fusion.4), kind=kOutput, calls=%fused_computation.112 | convolution fusion | flops 2420441088 | bytes 10657792 | tf_op jit(solution)/shard_map/lsd,lse->de/dot_general | solution.py:27
  215.5 8.0 %fusion.84 = bf16[1536,384]{1,0:T(8,128)(2,1)} fusion(bf16[8,256,1536]{2,1,0:T(8,128)(2,1)} %get-tuple-element.205, bf16[8,256,384]{2,1,0:T(8,128)(2,1)} %param.29, f32[8,384]{1,0:T(8,128)S(1)} %copy-done.19), kind=kOutput, calls=%fused_computation.113 | convolution fusion | flops 2418868224 | bytes 9056256 | tf_op jit(solution)/shard_map/lsd,lse->de/dot_general | solution.py:27
  223.6 6.2 %fusion.76 = (bf16[8,384]{1,0:T(8,128)(2,1)S(1)}, f32[8,256]{1,0:T(8,128)S(1)}, f32[8,256]{1,0:T(8,128)S(1)}, bf16[8,384]{1,0:T(8,128)(2,1)S(1)}, f32[8,256,384]{2,1,0:T(8,128)S(1)}) fusion(bf16[8,256,384]{2,1,0:T(8,128)(2,1)S(1)} %copy-done, f32[8,256]{1,0:T(8,128)S(1)} %add_rsqrt_fusion.1, f32[8,256]{1,0:T(8,128)S(1)} %broadcast_multiply_fusion.5, ...), kind=kOutput, calls=%fused_computation.91 | convolution fusion | flops 1833949184 | bytes 10379264 | tf_op jit(solution)/shard_map/lse,de->lsd/dot_general | solution.py:155
  229.9 3.1 multiply_reduce_fusion.3
  235.2 24.6 %reduce-scatter.12.cloned.1.call-done = bf16[96,1536]{1,0:T(8,128)(2,1)} async-done(((bf16[384,1536]{1,0:T(8,128)(2,1)}), bf16[96,1536]{1,0:T(8,128)(2,1)}) %reduce-scatter.12.cloned.1.call-update) | async-done | bytes 294928 | tf_op jit(solution)/shard_map/reduce_scatter | solution.py:185
  259.8 28.5 %reduce-scatter.14.cloned.1.call-done = bf16[384,384]{1,0:T(8,128)(2,1)} async-done(((bf16[1536,384]{1,0:T(8,128)(2,1)}), bf16[384,384]{1,0:T(8,128)(2,1)}) %reduce-scatter.14.cloned.1.call-update) | async-done | bytes 294928 | tf_op jit(solution)/shard_map/reduce_scatter | solution.py:191
  288.3 32.0 %reduce-scatter.6.cloned.1.call-done = bf16[96,2304]{1,0:T(8,128)(2,1)} async-done(((bf16[384,2304]{1,0:T(8,128)(2,1)}), bf16[96,2304]{1,0:T(8,128)(2,1)}) %reduce-scatter.6.cloned.1.call-update) | async-done | bytes 442384 | tf_op jit(solution)/shard_map/reduce_scatter | solution.py:167
  326.9 10.5 %all-reduce.12 = (bf16[2304]{0:T(1024)(128)(2,1)S(1)}, bf16[768]{0:T(1024)(128)(2,1)S(1)}, bf16[384]{0:T(512)(128)(2,1)S(1)}, bf16[1536]{0:T(1024)(128)(2,1)S(1)}, bf16[384]{0:T(512)(128)(2,1)S(1)}) all-reduce(bf16[2304]{0:T(1024)(128)(2,1)S(1)} %reduce_sum.227, ...), channel_id=4, replica_groups=mesh['rep'=8,'shard'=4] {'shard'}, use_global_device_ids=true, to_apply=%region_24.25.clone | all-reduce | flops 5376 | bytes 21504
  338.0 37.3 %all-reduce.10 = (bf16[4608]{0:T(1024)(128)(2,1)S(1)}, bf16[192]{0:T(256)(128)(2,1)S(1)}, bf16[96]{0:T(256)(128)(2,1)S(1)}, bf16[384]{0:T(512)(128)(2,1)S(1)}, bf16[96]{0:T(256)(128)(2,1)S(1)}) all-reduce(bf16[4608]{0:T(1024)(128)(2,1)S(1)} %dynamic-update-slice.4, ...), channel_id=2, replica_groups=mesh['rep'=8,'shard'=4] {'rep'}, use_global_device_ids=true, to_apply=%add.4 | all-reduce | flops 5376 | bytes 21504
  379.4 30.5 %all-reduce.16.cloned.1.call-done = (bf16[96,2304]{1,0:T(8,128)(2,1)}, bf16[96,1152]{1,0:T(8,128)(2,1)}, bf16[96,384]{1,0:T(8,128)(2,1)}, bf16[96,1536]{1,0:T(8,128)(2,1)}, bf16[384,384]{1,0:T(8,128)(2,1)}) async-done(((bf16[96,2304]{1,0:T(8,128)(2,1)}, bf16[96,1152]{1,0:T(8,128)(2,1)}, bf16[96,384]{1,0:T(8,128)(2,1)}, bf16[96,1536]{1,0:T(8,128)(2,1)}, bf16[384,384]{1,0:T(8,128)(2,1)}), ...) | async-done | bytes 1327120 | tf_op jit(solution)/shard_map/psum | solution.py:199
  (231 shorter events, 126.5 us)
Async XLA Ops:
  7.2 31.1 %copy-start = (bf16[8,256,384]{2,1,0:T(8,128)(2,1)S(1)}, bf16[8,256,384]{2,1,0:T(8,128)(2,1)}, u32[]{:S(2)}) copy-start(bf16[8,256,384]{2,1,0:T(8,128)(2,1)} %param.17) | copy-start | bytes 4718596
  7.2 32.0 %copy-start.15 = (bf16[96,384]{1,0:T(8,128)(2,1)S(1)}, bf16[96,384]{1,0:T(8,128)(2,1)}, u32[]{:S(2)}) copy-start(bf16[96,384]{1,0:T(8,128)(2,1)} %param.23) | copy-start | bytes 221188
  7.2 37.9 %copy-start.14 = (bf16[96,1152]{1,0:T(8,128)(2,1)S(1)}, bf16[96,1152]{1,0:T(8,128)(2,1)}, u32[]{:S(2)}) copy-start(bf16[96,1152]{1,0:T(8,128)(2,1)} %param.21) | copy-start | bytes 663556
  7.2 49.2 %copy-start.16 = (bf16[8,384]{1,0:T(8,128)(2,1)S(1)}, bf16[8,384]{1,0:T(8,128)(2,1)}, u32[]{:S(2)}) copy-start(bf16[8,384]{1,0:T(8,128)(2,1)} %param.18) | copy-start | bytes 18436
  7.2 49.2 %all-gather.6.cloned.1.call-start = ((), (), s32[]{:S(2)}) async-start(), calls=%async_computation.5 | async-start | bytes 2211840 | tf_op jit(solution)/shard_map/all_gather | solution.py:74
  8.0 92.7 %all-gather.8.cloned.1.call-start = ((), (), s32[]{:S(2)}) async-start(), calls=%async_computation.6 | async-start | bytes 1474560 | tf_op jit(solution)/shard_map/all_gather | solution.py:80
  8.7 103.0 %all-gather.10.cloned.1.call-start = ((), (), s32[]{:S(2)}) async-start(), calls=%async_computation.7 | async-start | bytes 1474560 | tf_op jit(solution)/shard_map/all_gather | solution.py:82
  9.4 225.7 %reduce-scatter.10.cloned.1.call-start = ((), (), s32[]{:S(2)}) async-start(), calls=%async_computation.10 | async-start | bytes 368640 | tf_op jit(solution)/shard_map/reduce_scatter | solution.py:179
  35.9 57.2 %copy-start.26 = (f32[384]{0:T(512)}, f32[384]{0:T(512)S(1)}, u32[]{:S(2)}) copy-start(f32[384]{0:T(512)S(1)} %convert_element_type.179) | copy-start | bytes 4612
  111.7 15.1 %copy-start.37 = (bf16[384,1536]{1,0:T(8,128)(2,1)S(1)}, bf16[384,1536]{1,0:T(8,128)(2,1)}, u32[]{:S(2)}) copy-start(bf16[384,1536]{1,0:T(8,128)(2,1)} %all-gather.8.cloned.1.call-done) | copy-start | bytes 3538948
  126.8 6.8 %copy-start.40 = (bf16[8,256,1536]{2,1,0:T(8,128)(2,1)S(1)}, bf16[8,256,1536]{2,1,0:T(8,128)(2,1)}, u32[]{:S(2)}) copy-start(bf16[8,256,1536]{2,1,0:T(8,128)(2,1)} %get-tuple-element.205) | copy-start | bytes 18874372
  150.3 84.8 %reduce-scatter.8.cloned.1.call-start = ((), (), s32[]{:S(2)}) async-start(), calls=%async_computation.9 | async-start | bytes 1105920 | tf_op jit(solution)/shard_map/reduce_scatter | solution.py:173
  207.5 8.0 %copy-start.19 = (f32[8,384]{1,0:T(8,128)S(1)}, f32[8,384]{1,0:T(8,128)}, u32[]{:S(2)}) copy-start(f32[8,384]{1,0:T(8,128)} %get-tuple-element.192) | copy-start | bytes 36868
  207.5 52.3 %reduce-scatter.12.cloned.1.call-start = ((), (), s32[]{:S(2)}) async-start(), calls=%async_computation.11 | async-start | bytes 1474560 | tf_op jit(solution)/shard_map/reduce_scatter | solution.py:185
  215.2 8.3 %copy-start.10 = (bf16[8,256,384]{2,1,0:T(8,128)(2,1)S(1)}, bf16[8,256,384]{2,1,0:T(8,128)(2,1)}, u32[]{:S(2)}) copy-start(bf16[8,256,384]{2,1,0:T(8,128)(2,1)} %copy.85) | copy-start | bytes 4718596
  215.2 73.0 %reduce-scatter.14.cloned.1.call-start = ((), (), s32[]{:S(2)}) async-start(), calls=%async_computation.12 | async-start | bytes 1474560 | tf_op jit(solution)/shard_map/reduce_scatter | solution.py:191
  223.5 96.8 %reduce-scatter.6.cloned.1.call-start = ((), (), s32[]{:S(2)}) async-start(), calls=%async_computation.8 | async-start | bytes 2211840 | tf_op jit(solution)/shard_map/reduce_scatter | solution.py:167
  233.0 87.3 %copy-start.38 = (u32[32]{0:T(128)S(1)}, u32[32]{0:T(128)}, u32[]{:S(2)}) copy-start(u32[32]{0:T(128)} %constant.105) | copy-start | bytes 388
  235.0 91.9 %copy-start.32 = (bf16[384]{0:T(512)(128)(2,1)S(1)}, bf16[384]{0:T(512)(128)(2,1)}, u32[]{:S(2)}) copy-start(bf16[384]{0:T(512)(128)(2,1)} %get-tuple-element.172) | copy-start | bytes 2308
  235.0 91.9 %copy-start.33 = (bf16[384]{0:T(512)(128)(2,1)S(1)}, bf16[384]{0:T(512)(128)(2,1)}, u32[]{:S(2)}) copy-start(bf16[384]{0:T(512)(128)(2,1)} %get-tuple-element.191) | copy-start | bytes 2308
  235.0 91.9 %copy-start.34 = (bf16[1536]{0:T(1024)(128)(2,1)S(1)}, bf16[1536]{0:T(1024)(128)(2,1)}, u32[]{:S(2)}) copy-start(bf16[1536]{0:T(1024)(128)(2,1)} %get-tuple-element.208) | copy-start | bytes 9220
  235.0 143.2 %copy-start.6 = (bf16[384,2304]{1,0:T(8,128)(2,1)S(1)}, bf16[384,2304]{1,0:T(8,128)(2,1)}, u32[]{:S(2)}) copy-start(bf16[384,2304]{1,0:T(8,128)(2,1)} %all-gather.6.cloned.1.call-done) | copy-start | bytes 5308420
  235.1 174.9 %all-reduce.16.cloned.1.call-start = ((), (), s32[]{:S(2)}) async-start(), calls=%async_computation.13 | async-start | bytes 2654208 | tf_op jit(solution)/shard_map/psum | solution.py:199
  409.9 7.1 %copy-start.13 = (bf16[384,384]{1,0:T(8,128)(2,1)S(1)}, bf16[384,384]{1,0:T(8,128)(2,1)}, u32[]{:S(2)}) copy-start(bf16[384,384]{1,0:T(8,128)(2,1)} %get-tuple-element.162) | copy-start | bytes 884740
  (29 other events, 119.7 us)
Sparse Core Ops, SparseCore 0:
  9.6 23.5 all-gather.5
  34.8 19.2 all-gather.7
  55.6 17.1 all-gather.9
  150.4 20.4 reduce-scatter.9
  207.6 23.9 reduce-scatter.7
  234.0 25.7 reduce-scatter.11
  262.5 25.7 reduce-scatter.13
  290.9 29.3 reduce-scatter.5
  324.8 85.0 all-reduce.15
